TPU v7x, 512 devices: a whole 4x8x8 slice. The times are simulated.
512 devices in a mesh: ctx: 64 (over y, z), tp: 8 (over x, core).
Axes of the slice: x: 4, y: 8, z: 8, core: 2. Of those that a mesh axis runs over, the one named last changes fastest.
Arguments:
- query: bfloat16 [8192, 8192], P('ctx', 'tp'), may hold values from -6 to 6
- keyed: bfloat16 [8192, 8192], P('ctx', 'tp'), may hold values from -6 to 6
- valued: bfloat16 [8192, 8192], P('ctx', 'tp'), may hold values from -6 to 6
- short_taps: float32 [3, 3, 8192], P(None, None, 'tp'), may hold values from -3.5 to 3.5
- rates: float32 [8, 8192], P(None, 'tp'), may hold values from 3.0517578e-05 to 0.1
- residues: float32 [8, 8192], P(None, 'tp'), may hold values from -1.5 to 1.5
- skip_gain: float32 [8192], P('tp'), may hold values from -1.6 to 1.6
- doc_ids: int32 [8192], P('ctx'), may hold values from 0 to 7, never falling along the last dimension, each value on 1 to 4096 neighbouring positions
Outputs:
- mixed: bfloat16 [8192, 8192], P('ctx', 'tp')
Inputs may be any that keep to these rules, and one draw needn't show every extreme that they name: doc_ids never falls along the sequence; each of the 8 documents holds 1 to 4096 consecutive tokens, one exactly 4096.
All inputs are finite; a program needn't handle non-finite values.
Results may differ from a plain program's by a relative error of at most 0.0065.
Values may be sent and summed in bfloat16 or wider, within the bound.
A program may use at most 128 MiB of HBM per device.

v0:
```python
import jax
import jax.numpy as jnp
from jax import lax
from jax.sharding import PartitionSpec as P


def shifted_2(value, axis, steps):
    count = lax.axis_size(axis)
    first, last = (max(0, -steps), min(count, count - steps))
    return lax.ppermute(value, axis, [(source, source + steps) for source in range(first, last)])


def short_conv(ext, ids_ext, taps):
    width = taps.shape[1] - 1
    length = ext.shape[1] - width
    total = jnp.zeros((ext.shape[0], length, ext.shape[2]), jnp.float32)
    for tap in range(taps.shape[1]):
        seg = ext[:, width - tap : width - tap + length]
        same = (ids_ext[width - tap : width - tap + length] == ids_ext[width:]).astype(jnp.float32)
        total = total + taps[:, tap][:, None, :] * seg * same[None, :, None]
    return total


def mode_terms_all(gated, ids, rates, residues):
    block, channels = gated.shape
    order = rates.shape[0]
    places = jnp.arange(block, dtype=jnp.float32)
    shifted = places - float(block // 2)
    lower = places[:, None] >= places[None, :]
    mask = (lower & (ids[:, None] == ids[None, :])).astype(jnp.float32)
    grow = jnp.exp(rates[None] * shifted[:, None, None])
    weighted = (grow * gated[:, None, :]).reshape(block, order * channels)
    summed = jnp.dot(mask, weighted, precision=lax.Precision.HIGHEST).reshape(
        block, order, channels
    )
    states = summed * jnp.exp(-rates[None] * shifted[:, None, None])
    long_part = jnp.sum(residues[None] * states, axis=1)
    return (long_part, states[block - 1])


def incoming(carry, ids, prev_last, rates, residues):
    block = ids.shape[0]
    places = jnp.arange(block, dtype=jnp.float32) + 1.0
    live = (ids == prev_last).astype(jnp.float32)
    total = jnp.zeros((block, rates.shape[1]), jnp.float32)
    for group in range(rates.shape[0] // 4):
        rate = rates[4 * group : 4 * group + 4]
        weight = residues[4 * group : 4 * group + 4] * carry[4 * group : 4 * group + 4]
        total = total + jnp.sum(weight[None] * jnp.exp(-rate[None] * places[:, None, None]), axis=1)
    return total * live[:, None]


def transition(ids, prev_last, rates):
    block = ids.shape[0]
    keep = ((ids[0] == prev_last) & (ids[0] == ids[block - 1])).astype(jnp.float32)
    return jnp.exp(-rates * block) * keep


def combine(earlier, later):
    return (earlier[0] * later[0], later[0] * earlier[1] + later[1])


def on_device(query, keyed, valued, short_taps, rates, residues, skip_gain, doc_ids):
    block, channels = query.shape
    width = short_taps.shape[1] - 1
    stacked = jnp.stack([query, keyed, valued])
    prev_rows, prev_ids = shifted_2(
        (stacked[:, block - width :], doc_ids[block - width :]), "ctx", 1
    )
    ext = jnp.concatenate([prev_rows, stacked], axis=1).astype(jnp.float32)
    ids_ext = jnp.concatenate([prev_ids, doc_ids])
    conv = short_conv(ext, ids_ext, short_taps)
    gated = (conv[1] * conv[2]).astype(jnp.bfloat16)
    gated_f = gated.astype(jnp.float32)
    n_ctx = lax.axis_size("ctx")
    group_width = channels // n_ctx
    whole = lax.all_to_all(gated, "ctx", split_axis=1, concat_axis=0, tiled=True)
    ids_all = lax.all_gather(doc_ids, "ctx", axis=0, tiled=True)
    offset = lax.axis_index("ctx") * group_width
    rate_sub = lax.dynamic_slice_in_dim(rates, offset, group_width, 1)
    resid_sub = lax.dynamic_slice_in_dim(residues, offset, group_width, 1)
    blocks_u = whole.reshape(n_ctx, block, group_width).astype(jnp.float32)
    blocks_ids = ids_all.reshape(n_ctx, block)
    prev_lasts = jnp.concatenate([jnp.zeros((1,), jnp.int32), blocks_ids[:-1, block - 1]])
    local_parts, ends = jax.vmap(lambda uu, ii: mode_terms_all(uu, ii, rate_sub, resid_sub))(
        blocks_u, blocks_ids
    )
    keeps = jax.vmap(lambda ii, pp: transition(ii, pp, rate_sub))(blocks_ids, prev_lasts)
    _, inclusive = lax.associative_scan(combine, (keeps, ends), axis=0)
    carries = jnp.concatenate([jnp.zeros_like(inclusive[:1]), inclusive[:-1]], axis=0)
    entering = jax.vmap(lambda cc, ii, pp: incoming(cc, ii, pp, rate_sub, resid_sub))(
        carries, blocks_ids, prev_lasts
    )
    grouped = (local_parts + entering).reshape(n_ctx * block, group_width)
    long_all = lax.all_to_all(grouped, "ctx", split_axis=0, concat_axis=1, tiled=True)
    return (conv[0] * (long_all + skip_gain[None] * gated_f)).astype(jnp.bfloat16)


def solution(mesh):
    return jax.shard_map(
        on_device,
        mesh=mesh,
        in_specs=(
            P("ctx", "tp"),
            P("ctx", "tp"),
            P("ctx", "tp"),
            P(None, None, "tp"),
            P(None, "tp"),
            P(None, "tp"),
            P("tp"),
            P("ctx"),
        ),
        out_specs=P("ctx", "tp"),
        check_vma=False,
    )
```

profile of v0, /device:TPU:6, one launch (start us, length us, event | category | flops | bytes accessed | tf_op | source)
XLA Modules:
  0.0 192.9 jit_solution(2154041682382078537)
XLA Ops:
  0.0 1.1 copy.45
  1.2 1.1 copy.44
  2.3 1.1 copy.43
  3.4 0.3 pad_maximum_fusion
  3.7 0.3 copy.46
  4.0 4.3 %collective-permute-start = (bf16[3,2,1024]{2,1,0:T(2,128)(2,1)S(1)}, bf16[3,2,1024]{2,1,0:T(2,128)(2,1)S(1)}, u32[]{:S(2)}, u32[]{:S(2)}) collective-permute-start(bf16[3,2,1024]{2,1,0:T(2,128)(2,1)S(1)} %copy.46), channel_id=1, source_target_pairs={{0,8},{8,16},{16,24},{24,32},{32,40},{40,48},{48,56},{56,64},{64,7... | collective-permute-start | bytes 36872 | tf_op jit(solution)/shard_map/ppermute | solution.py:10
  8.4 4.3 %collective-permute-start.1 = (s32[2]{0:T(128)S(1)}, s32[2]{0:T(128)S(1)}, u32[]{:S(2)}, u32[]{:S(2)}) collective-permute-start(s32[2]{0:T(128)S(1)} %slice.217), channel_id=1, source_target_pairs={{0,8},{8,16},{16,24},{24,32},{32,40},{40,48},{48,56},{56,64},{64,7... | collective-permute-start | bytes 32 | tf_op jit(solution)/shard_map/ppermute | solution.py:10
  12.7 0.8 multiply_exponential_fusion.4
  13.5 47.9 %all-gather = s32[64,1,128]{2,1,0:T(1,128)S(1)} all-gather(s32[1,1,128]{2,1,0:T(1,128)S(1)} %bitcast.48), channel_id=1, replica_groups=mesh['ctx'=64,'tp'=8] {'ctx'}, dimensions={0}, use_global_device_ids=true | all-gather | bytes 33280 | tf_op jit(solution)/shard_map/all_gather | solution.py:78
  61.4 0.2 slice_reduce_fusion
  61.6 0.2 slice_reduce_fusion.1
  62.5 0.4 copy.47
  63.0 0.6 maximum_convert_fusion
  63.6 2.3 %fusion.7 = f32[3,128,1024]{1,2,0:T(8,128)S(1)} fusion(f32[3,130,1024]{1,2,0:T(8,128)S(1)} %maximum_convert_fusion, f32[128]{0:T(128)S(1)} %get-tuple-element.36, f32[3,1024]{1,0:T(4,128)S(1)} %get-tuple-element.39, f32[128]{0:T(128)S(1)} %get-tuple-element.35, f32[3,1024]{1,0:T(4,128)S(1)} %get-tuple-element.40, f32[3,1024]{1,0:T(4,128)S(1)} %bitcast.47), kind=kLoop, calls=%fused_computation.13 | loop fusion | flops 2752512 | bytes 6329344 | tf_op jit(solution)/shard_map/add | solution.py:20
  65.9 0.8 fusion.10
  66.7 8.1 %all-to-all-start = ((bf16[128,64,16]{0,2,1:T(8,128)(2,1)}), bf16[128,64,16]{0,2,1:T(8,128)(2,1)S(1)}, u32[]{:S(2)}, u32[]{:S(2)}) async-start(bf16[128,64,16]{0,2,1:T(8,128)(2,1)} %bitcast.6), calls=%async_computation | async-start | bytes 524288 | tf_op jit(solution)/shard_map/all_to_all | solution.py:77
  75.0 0.2 multiply_exponential_fusion
  75.2 13.0 %all-to-all-done = bf16[128,64,16]{0,2,1:T(8,128)(2,1)S(1)} async-done(((bf16[128,64,16]{0,2,1:T(8,128)(2,1)}), bf16[128,64,16]{0,2,1:T(8,128)(2,1)S(1)}, u32[]{:S(2)}, u32[]{:S(2)}) %all-to-all-start) | async-done | bytes 262176 | tf_op jit(solution)/shard_map/all_to_all | solution.py:77
  88.3 0.6 bitcast_multiply_fusion
  88.9 6.1 %fusion = f32[64,128,128]{1,2,0:T(8,128)} fusion(f32[64,128,128]{1,2,0:T(8,128)S(1)} %bitcast_multiply_fusion, s32[64,128]{1,0:T(8,128)S(1)} %bitcast.46, pred[128,128]{1,0:T(8,128)(4,1)S(1)} %iota_compare_fusion), kind=kOutput, calls=%fused_computation.3 | convolution fusion | flops 1612709888 | bytes 8437760 | tf_op jit(solution)/shard_map/vmap()/dot_general | solution.py:33
  95.0 16.9 %copy.48 = f32[64,128,8,16]{3,2,1,0:T(8,128)} copy(f32[64,128,8,16]{1,3,2,0:T(8,128)} %bitcast.36) | data formatting | bytes 8388608 | tf_op jit(solution)/shard_map/vmap()/reshape | solution.py:33
  111.9 53.4 %multiply_reduce_fusion = (f32[64,128,16]{2,1,0:T(8,128)}, f32[64,128,8,16]{3,2,1,0:T(8,128)}) fusion(f32[8,16]{1,0:T(8,128)S(1)} %constant_dynamic-slice_fusion.1, f32[64,128,8,16]{3,2,1,0:T(8,128)} %copy.48, f32[128,8,16]{2,1,0:T(8,128)S(1)} %multiply_exponential_fusion), kind=kLoop, calls=%fused_computation | loop fusion | flops 3014656 | bytes 8978944 | tf_op jit(solution)/shard_map/vmap()/reduce_sum | solution.py:37
  165.3 1.0 slice_bitcast_fusion.1
  166.9 0.7 slice_bitcast_fusion.2
  167.9 2.8 %copy.49 = f32[64,128,16]{1,2,0:T(8,128)S(1)} copy(f32[64,128,16]{2,1,0:T(8,128)} %get-tuple-element.9) | data formatting | bytes 1048576 | tf_op jit(solution)/shard_map/vmap()/reduce_sum | solution.py:37
  170.7 0.2 pad.75
  171.0 0.2 pad.116
  171.3 0.6 multiply_reduce_fusion.2
  171.9 0.6 multiply_reduce_fusion.1
  172.7 19.1 %all_to_all.26 = f32[64,128,16]{1,2,0:T(8,128)S(1)} all-to-all(f32[64,128,16]{1,2,0:T(8,128)S(1)} %multiply_add_fusion), channel_id=1, replica_groups=mesh['ctx'=64,'tp'=8] {'ctx'}, dimensions={0} | all-to-all | bytes 1048576 | tf_op jit(solution)/shard_map/all_to_all | solution.py:95
  191.8 0.2 fusion.12
  192.1 0.9 copy.50
  (68 shorter events, 2.0 us)
Async XLA Ops:
  0.0 61.8 %copy-start = (f32[8,1024]{1,0:T(8,128)S(1)}, f32[8,1024]{1,0:T(8,128)}, u32[]{:S(2)}) copy-start(f32[8,1024]{1,0:T(8,128)} %param.13) | copy-start | bytes 98308
  0.0 8.3 %copy-start.3 = (s32[128]{0:T(128)S(1)}, s32[128]{0:T(128)}, u32[]{:S(2)}) copy-start(s32[128]{0:T(128)} %param.15) | copy-start | bytes 1540
  0.0 61.8 %copy-start.2 = (f32[3,3,1024]{2,1,0:T(4,128)S(1)}, f32[3,3,1024]{2,1,0:T(4,128)}, u32[]{:S(2)}) copy-start(f32[3,3,1024]{2,1,0:T(4,128)} %param.11) | copy-start | bytes 110596
  4.0 58.5 %collective-permute-start = (bf16[3,2,1024]{2,1,0:T(2,128)(2,1)S(1)}, bf16[3,2,1024]{2,1,0:T(2,128)(2,1)S(1)}, u32[]{:S(2)}, u32[]{:S(2)}) collective-permute-start(bf16[3,2,1024]{2,1,0:T(2,128)(2,1)S(1)} %copy.46), channel_id=1, source_target_pairs={{0,8},{8,16},{16,24},{24,32},{32,40},{40,48},{48,56},{56,64},{64,7... | collective-permute-start | bytes 36872 | tf_op jit(solution)/shard_map/ppermute | solution.py:10
  8.4 54.0 %collective-permute-start.1 = (s32[2]{0:T(128)S(1)}, s32[2]{0:T(128)S(1)}, u32[]{:S(2)}, u32[]{:S(2)}) collective-permute-start(s32[2]{0:T(128)S(1)} %slice.217), channel_id=1, source_target_pairs={{0,8},{8,16},{16,24},{24,32},{32,40},{40,48},{48,56},{56,64},{64,7... | collective-permute-start | bytes 32 | tf_op jit(solution)/shard_map/ppermute | solution.py:10
  66.7 21.6 %all-to-all-start = ((bf16[128,64,16]{0,2,1:T(8,128)(2,1)}), bf16[128,64,16]{0,2,1:T(8,128)(2,1)S(1)}, u32[]{:S(2)}, u32[]{:S(2)}) async-start(bf16[128,64,16]{0,2,1:T(8,128)(2,1)} %bitcast.6), calls=%async_computation | async-start | bytes 524288 | tf_op jit(solution)/shard_map/all_to_all | solution.py:77
  171.9 19.9 %copy-start.4 = (f32[1024]{0:T(1024)S(1)}, f32[1024]{0:T(1024)}, u32[]{:S(2)}) copy-start(f32[1024]{0:T(1024)} %param.14) | copy-start | bytes 12292
  172.6 20.4 %copy-start.1 = (f32[8,1024]{1,0:T(8,128)S(1)}, f32[8,1024]{1,0:T(8,128)}, u32[]{:S(2)}) copy-start(f32[8,1024]{1,0:T(8,128)} %param.13) | copy-start | bytes 98308
where the time goes:
time: 194 us; the launch traced here: 193 us
  blocking collectives  67 us (35%)
  other arithmetic  61.6 us (32%)
  local copies, waits for them, and re-layouts  27.9 us (14%)
  starting transfers between devices  16.7 us (9%)
  waiting for transfers between devices  13 us (7%)
  matrix products  6.12 us (3%)
    reduce_sum x1, other arithmetic, mode_terms_all(): long_part = jnp.sum(residues[None] * states, axis=1)  53.4 us
    all_gather x1, blocking collectives, on_device(): ids_all = lax.all_gather(doc_ids, 'ctx', axis=0, tiled=True)  47.9 us
    all_to_all x1, blocking collectives, on_device(): lax.all_to_all(grouped, 'ctx', split_axis=0, concat_axis=1, tiled=True)  19.1 us
    reshape x1, local copies, waits for them, and re-layouts, mode_terms_all(): jnp.dot(mask, weighted, precision=lax.Precision.HIGHEST)  16.9 us
    all_to_all x1, waiting for transfers between devices, on_device(): lax.all_to_all(gated, 'ctx', split_axis=1, concat_axis=0, tiled=True)  13 us
    ppermute x2, starting transfers between devices, shifted_2(): lax.ppermute(value, axis, [(source, source + steps) for source in range(f...  8.54 us
    all_to_all x1, starting transfers between devices, on_device(): lax.all_to_all(gated, 'ctx', split_axis=1, concat_axis=0, tiled=True)  8.13 us
    dot_general x1, matrix products, mode_terms_all(): jnp.dot(mask, weighted, precision=lax.Precision.HIGHEST)  6.12 us
  transfers between devices with their start and end apart: 3, of which 1 were waited for; matrix products, arithmetic and copies ran while one was open for 1% of the time, Pallas kernels for 0%

commit v1 on v0

v1 whole, which is shorter than its diff:
```python
import functools

import jax
import jax.numpy as jnp
from jax import lax
from jax.experimental import pallas as pl
from jax.experimental.pallas import tpu as pltpu
from jax.sharding import PartitionSpec as P

MESH = pl.DeviceIdType.MESH
F32 = jnp.float32
BF16 = jnp.bfloat16
ROW = 8
REACH = 4
LANES = 128
GROUPS = 8
STEP = 8
CHUNK = 16


def tree_sum(terms):
    while len(terms) > 1:
        terms = [a + b for a, b in zip(terms[::2], terms[1::2])] + terms[len(terms) & ~1 :]
    return terms[0]


def flag(cond):
    return jnp.where(cond, 1.0, 0.0).astype(F32)


def kernel(
    n_ctx, pitch,
    q_hbm, k_hbm, v_hbm, taps_hbm, rates_hbm, resid_hbm, skip_hbm, ids_hbm,
    out_hbm,
    raw, xs, taps_in, rates_in, resid_in, skip_in, ids,
    prm, taps, rate, resid,
    gated, base, live_q, out_x, out_raw,
    halo_out, halo_in, ends_out, ends_in, row_out, row_in, carry_out, carry_in,
    load_sem, store_sem, halo_send, halo_recv, ends_send, ends_recv, row_send, row_recv,
    carry_send, carry_recv,
):
    block = q_hbm.shape[0]
    modes = rates_hbm.shape[0]
    last = block - 1
    me = lax.axis_index("ctx")
    tp = lax.axis_index("tp")
    y, z = me // ROW, lax.rem(me, ROW)
    n_rows = n_ctx // ROW
    root = y * ROW

    def at(device):
        return (device, tp)

    barrier = pltpu.get_barrier_semaphore()

    def greet(device):
        pl.semaphore_signal(barrier, inc=1, device_id=at(device), device_id_type=MESH)

    @pl.when(z == 0)
    def _():
        for peer in range(1, ROW):
            greet(root + peer)
        for back in range(1, REACH + 1):
            @pl.when(y >= back)
            def _():
                greet(root - back * ROW)

    @pl.when(me > 0)
    def _():
        greet(me - 1)

    loads = [
        pltpu.make_async_copy(src, dst, load_sem.at[i])
        for i, (src, dst) in enumerate(
            [
                (k_hbm, raw.at[1]), (v_hbm, raw.at[2]), (q_hbm, raw.at[0]), (ids_hbm, ids),
                (rates_hbm, rates_in), (taps_hbm, taps_in), (resid_hbm, resid_in),
                (skip_hbm, skip_in),
            ]
        )
    ]
    for load in loads:
        load.start()

    for i in (4, 5, 6, 7):
        loads[i].wait()
    for j in range(GROUPS):
        cols = slice(j * LANES, (j + 1) * LANES)
        prm[pl.ds(j * 32, modes), :] = rates_in[:, cols]
        prm[pl.ds(j * 32 + 8, modes), :] = resid_in[:, cols]
        for s in range(3):
            for tap in range(3):
                prm[pl.ds(j * 32 + 16 + 3 * s + tap, 1), :] = taps_in[s, pl.ds(tap, 1), cols]
    for n in range(modes):
        rate[n] = prm[pl.ds(n, GROUPS, stride=32), :]
        resid[n] = prm[pl.ds(8 + n, GROUPS, stride=32), :]
    for i in range(9):
        taps[i] = prm[pl.ds(16 + i, GROUPS, stride=32), :]

    def spread(s):
        for j in range(GROUPS):
            xs[s, pl.ds(j * pitch, block), :] = raw[s, :, j * LANES : (j + 1) * LANES].astype(F32)

    def token(s, t):
        return xs[s, pl.ds(t, GROUPS, stride=pitch), :]

    loads[0].wait()
    spread(1)
    loads[1].wait()
    spread(2)
    loads[2].wait()
    spread(0)
    loads[3].wait()
    for s in range(3):
        halo_out[2 * s] = token(s, last - 1)
        halo_out[2 * s + 1] = token(s, last)
    halo_out[6] = jnp.full((GROUPS, LANES), ids[last - 1].astype(F32), F32)
    halo_out[7] = jnp.full((GROUPS, LANES), ids[last].astype(F32), F32)

    halo = pltpu.make_async_remote_copy(
        src_ref=halo_out, dst_ref=halo_in, send_sem=halo_send, recv_sem=halo_recv,
        device_id=at(lax.rem(me + 1, n_ctx)), device_id_type=MESH,
    )

    def enter():
        rows_ahead = jnp.minimum(REACH, n_rows - 1 - y)
        expected = jnp.where(me < n_ctx - 1, 1, 0) + jnp.where(z == 0, rows_ahead, 1)
        pl.semaphore_wait(barrier, expected)

        @pl.when(me < n_ctx - 1)
        def _():
            halo.start()

    late = (z == 0) | (z == 3)

    @pl.when(jnp.logical_not(late))
    def _():
        enter()

    def ends_step(i, carry):
        k1, k2, v1, v2, *state = carry
        decay = [jnp.exp(-rate[n]) for n in range(modes)]
        t0 = i * STEP
        for d in range(STEP):
            t = t0 + d
            here = ids[t]
            same1 = flag(here == ids[jnp.maximum(t - 1, 0)])
            same2 = flag(here == ids[jnp.maximum(t - 2, 0)])
            ends = flag((here == ids[last]) & (t >= 2))
            k0, v0 = token(1, t), token(2, t)
            kc = taps[3] * k0 + taps[4] * (k1 * same1) + taps[5] * (k2 * same2)
            vc = taps[6] * v0 + taps[7] * (v1 * same1) + taps[8] * (v2 * same2)
            g = (kc * vc).astype(BF16).astype(F32)
            gated[t] = g
            g = g * ends
            state = [decay[n] * state[n] + g for n in range(modes)]
            k1, k2, v1, v2 = k0, k1, v0, v1
        return (k1, k2, v1, v2, *state)

    zero = jnp.zeros((GROUPS, LANES), F32)
    _, _, _, _, *state = lax.fori_loop(0, block // STEP, ends_step, (zero,) * (4 + modes))
    for n in range(modes):
        ends_out[n] = state[n]

    @pl.when(late)
    def _():
        enter()

    @pl.when(me > 0)
    def _():
        halo.wait_recv()

    @pl.when(me == 0)
    def _():
        halo_in[...] = jnp.full(halo_in.shape, -1.0, F32)

    id0, id1 = ids[0].astype(F32), ids[1].astype(F32)
    before2, before1 = halo_in[6], halo_in[7]
    same_01 = flag(ids[0] == ids[1])
    m0_1, m0_2 = flag(before1 == id0), flag(before2 == id0)
    m1_2 = flag(before1 == id1)

    def conv01(s):
        far, near = halo_in[2 * s], halo_in[2 * s + 1]
        x0, x1 = token(s, 0), token(s, 1)
        a, b, c = taps[3 * s], taps[3 * s + 1], taps[3 * s + 2]
        return (
            a * x0 + b * (near * m0_1) + c * (far * m0_2),
            a * x1 + b * (x0 * same_01) + c * (near * m1_2),
        )

    k_0, k_1 = conv01(1)
    v_0, v_1 = conv01(2)
    g0 = (k_0 * v_0).astype(BF16).astype(F32)
    g1 = (k_1 * v_1).astype(BF16).astype(F32)
    gated[0] = g0
    gated[1] = g1
    ends01 = flag(ids[1] == ids[last])
    for n in range(modes):
        first = jnp.exp(-rate[n]) * (g0 * same_01) + g1
        ends_out[n] += jnp.exp(-rate[n] * float(block - 2)) * (first * ends01)
    ends_out[modes] = m0_1 * flag(ids[0] == ids[last])

    to_root = pltpu.make_async_remote_copy(
        src_ref=ends_out, dst_ref=ends_in.at[lax.rem(z + ROW - 1, ROW)], send_sem=ends_send,
        recv_sem=ends_recv, device_id=at(root), device_id_type=MESH,
    )

    @pl.when(z > 0)
    def _():
        to_root.start()

    q_0, q_1 = conv01(0)

    def local_step(i, carry):
        q1, q2, *state = carry
        decay = [jnp.exp(-rate[n]) for n in range(modes)]
        weight = [resid[n] for n in range(modes)]
        t0 = i * STEP
        for d in range(STEP):
            t = t0 + d
            here = ids[t]
            same1 = flag(here == ids[jnp.maximum(t - 1, 0)])
            same2 = flag(here == ids[jnp.maximum(t - 2, 0)])
            q0 = token(0, t)
            qc = taps[0] * q0 + taps[1] * (q1 * same1) + taps[2] * (q2 * same2)
            if d < 2:
                qc = jnp.where(t == d, (q_0, q_1)[d], qc)
            g = gated[t]
            state = [decay[n] * (state[n] * same1) + g for n in range(modes)]
            long = tree_sum([weight[n] * state[n] for n in range(modes)])
            base[t] = qc * (long + skip_in[...] * g)
            live_q[t] = qc * flag(before1 == here.astype(F32))
            q1, q2 = q0, q1
        return (q1, q2, *state)

    lax.fori_loop(0, block // STEP, local_step, (zero,) * (2 + modes))

    row_size = float(ROW * block)

    def row_copy(back):
        return pltpu.make_async_remote_copy(
            src_ref=row_out, dst_ref=row_in.at[back - 1], send_sem=row_send.at[back - 1],
            recv_sem=row_recv.at[back - 1], device_id=at(lax.rem(me + back * ROW, n_ctx)),
            device_id_type=MESH,
        )

    def carry_copy(peer):
        return pltpu.make_async_remote_copy(
            src_ref=carry_out.at[peer - 1], dst_ref=carry_in, send_sem=carry_send,
            recv_sem=carry_recv, device_id=at(root + peer), device_id_type=MESH,
        )

    @pl.when(z == 0)
    def _():
        pltpu.make_async_remote_copy(
            src_ref=ends_in, dst_ref=ends_in, send_sem=ends_send, recv_sem=ends_recv,
            device_id=at(root), device_id_type=MESH,
        ).wait_recv()
        hop = [jnp.exp(-rate[n] * float(block)) for n in range(modes)]
        total = [ends_out[n] for n in range(modes)]
        keep = ends_out[modes]
        for peer in range(1, ROW):
            k = ends_in[peer - 1, modes]
            keep = keep * k
            total = [total[n] * (hop[n] * k) + ends_in[peer - 1, n] for n in range(modes)]
        for n in range(modes):
            row_out[n] = total[n]
        row_out[modes] = keep
        for back in range(1, REACH + 1):
            @pl.when(y + back < n_rows)
            def _():
                row_copy(back).start()

        carry_in[...] = jnp.zeros(carry_in.shape, F32)
        for back in range(REACH, 0, -1):
            @pl.when(y >= back)
            def _():
                row_copy(back).wait_recv()
                k = row_in[back - 1, modes]
                for n in range(modes):
                    decay = jnp.exp(-rate[n] * row_size) * k
                    carry_in[n] = decay * carry_in[n] + row_in[back - 1, n]

        now = [carry_in[n] for n in range(modes)]
        for peer in range(1, ROW):
            src = ends_out if peer == 1 else ends_in.at[peer - 2]
            k = src[modes]
            now = [now[n] * (hop[n] * k) + src[n] for n in range(modes)]
            for n in range(modes):
                carry_out[peer - 1, n] = now[n]
            carry_copy(peer).start()

    @pl.when(z > 0)
    def _():
        carry_copy(1).wait_recv()

    def store(c):
        rows = pl.ds(pl.multiple_of(c * CHUNK, CHUNK), CHUNK)
        return pltpu.make_async_copy(out_raw.at[rows], out_hbm.at[rows], store_sem)

    def out_step(c, part):
        decay = [jnp.exp(-rate[n]) for n in range(modes)]
        for d in range(CHUNK):
            t = c * CHUNK + d
            part = [decay[n] * part[n] for n in range(modes)]
            out_x[pl.ds(t, GROUPS, stride=pitch), :] = base[t] + live_q[t] * tree_sum(list(part))
        for j in range(GROUPS):
            rows = pl.ds(pl.multiple_of(c * CHUNK, CHUNK), CHUNK)
            piece = out_x[pl.ds(j * pitch + pl.multiple_of(c * CHUNK, CHUNK), CHUNK), :]
            out_raw[rows, j * LANES : (j + 1) * LANES] = piece.astype(BF16)
        store(c).start()
        return part

    lax.fori_loop(
        0, block // CHUNK, out_step, [resid[n] * carry_in[n] for n in range(modes)]
    )

    pltpu.make_async_copy(out_raw, out_hbm, store_sem).wait()

    @pl.when(me < n_ctx - 1)
    def _():
        halo.wait_send()

    @pl.when(z > 0)
    def _():
        to_root.wait_send()

    @pl.when(z == 0)
    def _():
        for back in range(1, REACH + 1):
            @pl.when(y + back < n_rows)
            def _():
                row_copy(back).wait_send()
        pltpu.make_async_remote_copy(
            src_ref=carry_out, dst_ref=carry_out, send_sem=carry_send, recv_sem=carry_recv,
            device_id=at(root), device_id_type=MESH,
        ).wait_send()


def on_device(n_ctx, query, keyed, valued, short_taps, rates, residues, skip_gain, doc_ids):
    block, channels = query.shape
    modes = rates.shape[0]
    assert channels == GROUPS * LANES and block % CHUNK == 0 and modes == 8
    pitch = block + 8
    tile = (GROUPS, LANES)
    dma = pltpu.SemaphoreType.DMA
    any_space = pl.BlockSpec(memory_space=pl.ANY)
    return pl.pallas_call(
        functools.partial(kernel, n_ctx, pitch),
        out_shape=jax.ShapeDtypeStruct(query.shape, BF16),
        in_specs=[any_space] * 8,
        out_specs=any_space,
        scratch_shapes=[
            pltpu.VMEM((3, block, channels), BF16),
            pltpu.VMEM((3, GROUPS * pitch, LANES), F32),
            pltpu.VMEM(short_taps.shape, F32),
            pltpu.VMEM(rates.shape, F32),
            pltpu.VMEM(residues.shape, F32),
            pltpu.VMEM(tile, F32),
            pltpu.SMEM((block,), jnp.int32),
            pltpu.VMEM((GROUPS * 32, LANES), F32),
            pltpu.VMEM((9, *tile), F32),
            pltpu.VMEM((modes, *tile), F32),
            pltpu.VMEM((modes, *tile), F32),
            pltpu.VMEM((block, *tile), F32),
            pltpu.VMEM((block, *tile), F32),
            pltpu.VMEM((block, *tile), F32),
            pltpu.VMEM((GROUPS * pitch, LANES), F32),
            pltpu.VMEM((block, channels), BF16),
            pltpu.VMEM((8, *tile), F32),
            pltpu.VMEM((8, *tile), F32),
            pltpu.VMEM((modes + 1, *tile), F32),
            pltpu.VMEM((ROW - 1, modes + 1, *tile), F32),
            pltpu.VMEM((modes + 1, *tile), F32),
            pltpu.VMEM((REACH, modes + 1, *tile), F32),
            pltpu.VMEM((ROW - 1, modes, *tile), F32),
            pltpu.VMEM((modes, *tile), F32),
            dma((8,)),
            dma, dma, dma, dma, dma,
            dma((REACH,)),
            dma((REACH,)),
            dma, dma,
        ],
        compiler_params=pltpu.CompilerParams(
            collective_id=0, has_side_effects=True, vmem_limit_bytes=32 * 1024 * 1024
        ),
    )(
        query, keyed, valued, short_taps, rates, residues,
        skip_gain.reshape(tile), doc_ids,
    )


def solution(mesh):
    return jax.shard_map(
        functools.partial(on_device, mesh.shape["ctx"]),
        mesh=mesh,
        in_specs=(
            P("ctx", "tp"),
            P("ctx", "tp"),
            P("ctx", "tp"),
            P(None, None, "tp"),
            P(None, "tp"),
            P(None, "tp"),
            P("tp"),
            P("ctx"),
        ),
        out_specs=P("ctx", "tp"),
        check_vma=False,
    )
```

time: 194 us -> 34.3 us (0.18)
  the two profiles are of different devices: /device:TPU:6 before, /device:TPU:54 now
where the time goes in v1:
time: 34.3 us; the launch traced here: 33.9 us
  Pallas kernels  26.6 us (78%)
  local copies, waits for them, and re-layouts  7.21 us (21%)
    pallas_call x1, Pallas kernels, on_device(): pl.pallas_call(functools.partial(kernel, n_ctx, pitch), out_shape=jax.Sha...  26.6 us
    unnamed x17, local copies, waits for them, and re-layouts  7.21 us

profile of v1, /device:TPU:54, one launch (start us, length us, event | category | flops | bytes accessed | tf_op | source)
XLA Modules:
  0.0 33.9 jit_solution(9967731997258258813)
XLA Ops:
  0.0 0.0 copy-start.7
  0.0 0.7 %copy-done.7 = s32[128]{0:T(128)S(1)} copy-done((s32[128]{0:T(128)S(1)}, s32[128]{0:T(128)}, u32[]{:S(2)}) %copy-start.7) | copy-done | bytes 536
  0.7 0.0 copy-start
  0.7 0.9 %copy-done = bf16[128,1024]{1,0:T(8,128)(2,1)S(1)} copy-done((bf16[128,1024]{1,0:T(8,128)(2,1)S(1)}, bf16[128,1024]{1,0:T(8,128)(2,1)}, u32[]{:S(2)}) %copy-start) | copy-done | bytes 262168
  1.6 0.0 copy-start.1
  1.6 0.9 %copy-done.1 = bf16[128,1024]{1,0:T(8,128)(2,1)S(1)} copy-done((bf16[128,1024]{1,0:T(8,128)(2,1)S(1)}, bf16[128,1024]{1,0:T(8,128)(2,1)}, u32[]{:S(2)}) %copy-start.1) | copy-done | bytes 262168
  2.6 0.0 copy-start.2
  2.6 0.9 %copy-done.2 = bf16[128,1024]{1,0:T(8,128)(2,1)S(1)} copy-done((bf16[128,1024]{1,0:T(8,128)(2,1)S(1)}, bf16[128,1024]{1,0:T(8,128)(2,1)}, u32[]{:S(2)}) %copy-start.2) | copy-done | bytes 262168
  3.5 0.0 copy-start.3
  3.5 0.8 %copy-done.3 = f32[3,3,1024]{2,1,0:T(4,128)S(1)} copy-done((f32[3,3,1024]{2,1,0:T(4,128)S(1)}, f32[3,3,1024]{2,1,0:T(4,128)}, u32[]{:S(2)}) %copy-start.3) | copy-done | bytes 36888
  4.3 0.0 copy-start.4
  4.3 0.8 %copy-done.4 = f32[8,1024]{1,0:T(8,128)S(1)} copy-done((f32[8,1024]{1,0:T(8,128)S(1)}, f32[8,1024]{1,0:T(8,128)}, u32[]{:S(2)}) %copy-start.4) | copy-done | bytes 32792
  5.1 0.0 copy-start.5
  5.1 0.8 %copy-done.5 = f32[8,1024]{1,0:T(8,128)S(1)} copy-done((f32[8,1024]{1,0:T(8,128)S(1)}, f32[8,1024]{1,0:T(8,128)}, u32[]{:S(2)}) %copy-start.5) | copy-done | bytes 32792
  5.8 0.0 copy-start.6
  5.8 0.7 %copy-done.6 = f32[1024]{0:T(1024)S(1)} copy-done((f32[1024]{0:T(1024)S(1)}, f32[1024]{0:T(1024)}, u32[]{:S(2)}) %copy-start.6) | copy-done | bytes 4120
  6.5 26.6 %shard_map.82 = bf16[128,1024]{1,0:T(8,128)(2,1)S(1)} custom-call(bf16[128,1024]{1,0:T(8,128)(2,1)S(1)} %copy-done, bf16[128,1024]{1,0:T(8,128)(2,1)S(1)} %copy-done.1, bf16[128,1024]{1,0:T(8,128)(2,1)S(1)} %copy-done.2, f32[3,3,1024]{2,1,0:T(4,128)S(1)} %copy-done.3, f32[8,1024]{1,0:T(8,128)S(1)} %copy-done.4, f32[8,1024]{1,0:T(8,128)S(1)} %copy-done.5, ...), custom_call_target="tpu_custom_call" | custom-call | tf_op jit(solution)/shard_map/pallas_call | solution.py:349
  33.2 0.7 %copy.10 = bf16[128,1024]{1,0:T(8,128)(2,1)} copy(bf16[128,1024]{1,0:T(8,128)(2,1)S(1)} %shard_map.82) | data formatting | bytes 524288
Async XLA Ops:
  0.0 0.7 %copy-start.7 = (s32[128]{0:T(128)S(1)}, s32[128]{0:T(128)}, u32[]{:S(2)}) copy-start(s32[128]{0:T(128)} %ids_hbm.1) | copy-start | bytes 1540
  0.7 0.9 %copy-start = (bf16[128,1024]{1,0:T(8,128)(2,1)S(1)}, bf16[128,1024]{1,0:T(8,128)(2,1)}, u32[]{:S(2)}) copy-start(bf16[128,1024]{1,0:T(8,128)(2,1)} %q_hbm.1) | copy-start | bytes 786436
  1.6 0.9 %copy-start.1 = (bf16[128,1024]{1,0:T(8,128)(2,1)S(1)}, bf16[128,1024]{1,0:T(8,128)(2,1)}, u32[]{:S(2)}) copy-start(bf16[128,1024]{1,0:T(8,128)(2,1)} %k_hbm.1) | copy-start | bytes 786436
  2.6 0.9 %copy-start.2 = (bf16[128,1024]{1,0:T(8,128)(2,1)S(1)}, bf16[128,1024]{1,0:T(8,128)(2,1)}, u32[]{:S(2)}) copy-start(bf16[128,1024]{1,0:T(8,128)(2,1)} %v_hbm.1) | copy-start | bytes 786436
  3.5 0.8 %copy-start.3 = (f32[3,3,1024]{2,1,0:T(4,128)S(1)}, f32[3,3,1024]{2,1,0:T(4,128)}, u32[]{:S(2)}) copy-start(f32[3,3,1024]{2,1,0:T(4,128)} %taps_hbm.1) | copy-start | bytes 110596
  4.3 0.8 %copy-start.4 = (f32[8,1024]{1,0:T(8,128)S(1)}, f32[8,1024]{1,0:T(8,128)}, u32[]{:S(2)}) copy-start(f32[8,1024]{1,0:T(8,128)} %rates_hbm.1) | copy-start | bytes 98308
  5.1 0.8 %copy-start.5 = (f32[8,1024]{1,0:T(8,128)S(1)}, f32[8,1024]{1,0:T(8,128)}, u32[]{:S(2)}) copy-start(f32[8,1024]{1,0:T(8,128)} %resid_hbm.1) | copy-start | bytes 98308
  5.8 0.7 %copy-start.6 = (f32[1024]{0:T(1024)S(1)}, f32[1024]{0:T(1024)}, u32[]{:S(2)}) copy-start(f32[1024]{0:T(1024)} %param.14) | copy-start | bytes 12292

commit v2 on v1

v2 whole, which is shorter than its diff:
```python
import functools

import jax
import jax.numpy as jnp
from jax import lax
from jax.experimental import pallas as pl
from jax.experimental.pallas import tpu as pltpu
from jax.sharding import PartitionSpec as P

MESH = pl.DeviceIdType.MESH
F32 = jnp.float32
BF16 = jnp.bfloat16
ROW = 8
REACH = 4
LANES = 128
GROUPS = 8
STEP = 8
CHUNK = 16
SPLIT = 4


def tree_sum(terms):
    while len(terms) > 1:
        terms = [a + b for a, b in zip(terms[::2], terms[1::2])] + terms[len(terms) & ~1 :]
    return terms[0]


def flag(cond):
    return jnp.where(cond, 1.0, 0.0).astype(F32)


def kernel(
    n_ctx, pitch,
    q_hbm, k_hbm, v_hbm, taps_hbm, rates_hbm, resid_hbm, skip_hbm, ids_hbm,
    out,
    raw, xs, taps_in, rates_in, resid_in, skip_in, ids,
    prm, taps, rate, resid,
    gated, base, live_q, out_x,
    tail_out, tail_in, tail_q_out, tail_q_in, head_out, head_in,
    ends_out, ends_in, relay, row_out, row_in, carry_out, carry_in,
    load_sem, tail_sems, tail_q_sems, head_sems, lift_sems, forward_send, ends_sems,
    row_send, row_recv, carry_sems,
):
    block = q_hbm.shape[0]
    modes = rates_hbm.shape[0]
    last = block - 1
    me = lax.axis_index("ctx")
    tp = lax.axis_index("tp")
    y, z = me // ROW, lax.rem(me, ROW)
    n_rows = n_ctx // ROW
    root = y * ROW

    def at(device):
        return (device, tp)

    def remote(src, dst, send, recv, device):
        return pltpu.make_async_remote_copy(
            src_ref=src, dst_ref=dst, send_sem=send, recv_sem=recv,
            device_id=at(device), device_id_type=MESH,
        )

    barrier = pltpu.get_barrier_semaphore()

    def greet(device):
        pl.semaphore_signal(barrier, inc=1, device_id=at(device), device_id_type=MESH)

    @pl.when(z == 0)
    def _():
        for peer in range(1, ROW):
            if peer != SPLIT:
                greet(root + peer)
        for back in range(1, REACH + 1):
            @pl.when(y >= back)
            def _():
                greet(root - back * ROW)

    @pl.when(z == SPLIT - 1)
    def _():
        greet(me + 1)

    @pl.when(me > 0)
    def _():
        greet(me - 1)

    loads = [
        pltpu.make_async_copy(src, dst, load_sem.at[i])
        for i, (src, dst) in enumerate(
            [
                (k_hbm, raw.at[1]), (v_hbm, raw.at[2]), (ids_hbm, ids), (rates_hbm, rates_in),
                (taps_hbm, taps_in), (q_hbm, raw.at[0]), (resid_hbm, resid_in),
                (skip_hbm, skip_in),
            ]
        )
    ]
    for load in loads:
        load.start()

    def spread(s):
        for j in range(GROUPS):
            xs[s, pl.ds(j * pitch, block), :] = raw[s, :, j * LANES : (j + 1) * LANES].astype(F32)

    def token(s, t):
        return xs[s, pl.ds(t, GROUPS, stride=pitch), :]

    def splat(value):
        return jnp.full((GROUPS, LANES), value.astype(F32), F32)

    def put(ref, i, first, second):
        ref[i] = jnp.concatenate([first, second], axis=0).astype(BF16)

    def get(ref, i):
        both = ref[i].astype(F32)
        return both[:GROUPS], both[GROUPS:]

    loads[0].wait()
    spread(1)
    loads[1].wait()
    spread(2)
    loads[2].wait()
    id_0, id_1, id_end = splat(ids[0]), splat(ids[1]), splat(ids[last])
    for s in (1, 2):
        put(tail_out, s - 1, token(s, last - 1), token(s, last))
        put(head_out, s - 1, token(s, 0), token(s, 1))
    put(tail_out, 2, splat(ids[last - 1]), id_end)
    put(head_out, 2, id_0, id_1)
    put(head_out, 3, id_end, id_end)

    following = lax.rem(me + 1, n_ctx)
    tail = remote(tail_out, tail_in, tail_sems.at[0], tail_sems.at[1], following)
    tail_q = remote(tail_q_out, tail_q_in, tail_q_sems.at[0], tail_q_sems.at[1], following)

    def enter():
        rows_ahead = jnp.minimum(REACH, n_rows - 1 - y)
        expected = jnp.where(me < n_ctx - 1, 1, 0) + jnp.where(z == 0, rows_ahead, 1)
        pl.semaphore_wait(barrier, expected)

        @pl.when(me < n_ctx - 1)
        def _():
            tail.start()

    late = (z == 0) | (z == SPLIT - 1)

    @pl.when(jnp.logical_not(late))
    def _():
        enter()

    loads[3].wait()
    loads[4].wait()
    for j in range(GROUPS):
        cols = slice(j * LANES, (j + 1) * LANES)
        prm[pl.ds(j * 32, modes), :] = rates_in[:, cols]
        for s in range(3):
            for tap in range(3):
                prm[pl.ds(j * 32 + 16 + 3 * s + tap, 1), :] = taps_in[s, pl.ds(tap, 1), cols]
    for n in range(modes):
        rate[n] = prm[pl.ds(n, GROUPS, stride=32), :]
    for i in range(9):
        taps[i] = prm[pl.ds(16 + i, GROUPS, stride=32), :]

    def ends_step(i, carry):
        k1, k2, v1, v2, *state = carry
        decay = [jnp.exp(-rate[n]) for n in range(modes)]
        t0 = i * STEP
        for d in range(STEP):
            t = t0 + d
            here = ids[t]
            same1 = flag(here == ids[jnp.maximum(t - 1, 0)])
            same2 = flag(here == ids[jnp.maximum(t - 2, 0)])
            ends = flag((here == ids[last]) & (t >= 2))
            k0, v0 = token(1, t), token(2, t)
            kc = taps[3] * k0 + taps[4] * (k1 * same1) + taps[5] * (k2 * same2)
            vc = taps[6] * v0 + taps[7] * (v1 * same1) + taps[8] * (v2 * same2)
            g = (kc * vc).astype(BF16).astype(F32)
            gated[t] = g
            g = g * ends
            state = [decay[n] * state[n] + g for n in range(modes)]
            k1, k2, v1, v2 = k0, k1, v0, v1
        return (k1, k2, v1, v2, *state)

    zero = jnp.zeros((GROUPS, LANES), F32)
    _, _, _, _, *state = lax.fori_loop(0, block // STEP, ends_step, (zero,) * (4 + modes))
    for n in range(modes):
        ends_out[n] = state[n]
    ends_out[modes] = zero

    @pl.when(late)
    def _():
        enter()

    lifter = root + SPLIT - 1
    head = remote(head_out, head_in, head_sems.at[0], head_sems.at[1], lifter)
    lift = remote(ends_out, relay, lift_sems.at[0], lift_sems.at[1], lifter)
    forward = remote(relay, ends_in.at[SPLIT - 1], forward_send, ends_sems.at[1], root)
    slot = lax.rem(z + ROW - 1, ROW)
    ends = remote(ends_out, ends_in.at[slot], ends_sems.at[0], ends_sems.at[1], root)

    @pl.when(z == SPLIT)
    def _():
        head.start()
        lift.start()

    def first_two(s, before, x0, x1, before_ids, id0, id1):
        far, near = before
        id_far, id_near = before_ids
        a, b, c = taps[3 * s], taps[3 * s + 1], taps[3 * s + 2]
        return (
            a * x0 + b * (near * flag(id_near == id0)) + c * (far * flag(id_far == id0)),
            a * x1 + b * (x0 * flag(id0 == id1)) + c * (near * flag(id_near == id1)),
        )

    def first_gated(tail_ref, xk, xv, id0, id1):
        before_ids = get(tail_ref, 2)
        k = first_two(1, get(tail_ref, 0), *xk, before_ids, id0, id1)
        v = first_two(2, get(tail_ref, 1), *xv, before_ids, id0, id1)
        return [(a * b).astype(BF16).astype(F32) for a, b in zip(k, v)]

    def add_first(ref, g, id_near, id0, id1, end_id):
        joined, ending = flag(id0 == id1), flag(id1 == end_id)
        for n in range(modes):
            first = jnp.exp(-rate[n]) * (g[0] * joined) + g[1]
            ref[n] += jnp.exp(-rate[n] * float(block - 2)) * (first * ending)
        ref[modes] = flag(id_near == id0) * flag(id0 == end_id)

    def own_first():
        _, near_id = get(tail_in, 2)
        xk, xv = [(token(s, 0), token(s, 1)) for s in (1, 2)]
        gated[0], gated[1] = g = first_gated(tail_in, xk, xv, id_0, id_1)
        return g, near_id, id_0, id_1, id_end

    prompt = (z != 0) & (z != SPLIT)

    @pl.when(prompt)
    def _():
        tail.wait_recv()
        add_first(ends_out, *own_first())
        ends.start()

    loads[5].wait()
    spread(0)
    put(tail_q_out, 0, token(0, last - 1), token(0, last))

    @pl.when(me < n_ctx - 1)
    def _():
        tail_q.start()

    loads[6].wait()
    loads[7].wait()
    for j in range(GROUPS):
        prm[pl.ds(j * 32 + 8, modes), :] = resid_in[:, j * LANES : (j + 1) * LANES]
    for n in range(modes):
        resid[n] = prm[pl.ds(8 + n, GROUPS, stride=32), :]

    def local_step(i, carry):
        q1, q2, *state = carry
        decay = [jnp.exp(-rate[n]) for n in range(modes)]
        weight = [resid[n] for n in range(modes)]
        t0 = i * STEP
        for d in range(STEP):
            t = t0 + d
            here = ids[t]
            same1 = flag(here == ids[jnp.maximum(t - 1, 0)])
            same2 = flag(here == ids[jnp.maximum(t - 2, 0)])
            q0 = token(0, t)
            qc = taps[0] * q0 + taps[1] * (q1 * same1) + taps[2] * (q2 * same2)
            g = gated[t]
            if d < 2:
                g = g * flag(t >= 2)
            state = [decay[n] * (state[n] * same1) + g for n in range(modes)]
            long = tree_sum([weight[n] * state[n] for n in range(modes)])
            base[t] = qc * (long + skip_in[...] * g)
            live_q[t] = qc * flag(here == ids[1])
            q1, q2 = q0, q1
        return (q1, q2, *state)

    lax.fori_loop(0, block // STEP, local_step, (zero,) * (2 + modes))

    @pl.when((z == SPLIT) | ((z == 0) & (me > 0)))
    def _():
        tail.wait_recv()

    @pl.when(me == 0)
    def _():
        tail_in[...] = jnp.full(tail_in.shape, -1.0, BF16)
        tail_q_in[...] = jnp.zeros(tail_q_in.shape, BF16)

    @pl.when(z == 0)
    def _():
        add_first(ends_out, *own_first())

    @pl.when(z == SPLIT)
    def _():
        own_first()

    @pl.when(z == SPLIT - 1)
    def _():
        head.wait_recv()
        lift.wait_recv()
        (head_0, head_1), (head_end, _) = get(head_in, 2), get(head_in, 3)
        first = first_gated(tail_out, get(head_in, 0), get(head_in, 1), head_0, head_1)
        add_first(relay, first, id_end, head_0, head_1, head_end)
        forward.start()

    @pl.when(me > 0)
    def _():
        tail_q.wait_recv()

    row_size = float(ROW * block)

    def row_copy(back):
        return remote(
            row_out, row_in.at[back - 1], row_send.at[back - 1], row_recv.at[back - 1],
            lax.rem(me + back * ROW, n_ctx),
        )

    def carry_copy(peer):
        return remote(
            carry_out.at[peer - 1], carry_in, carry_sems.at[0], carry_sems.at[1], root + peer
        )

    def all_of(ref, sems):
        return remote(ref, ref, sems.at[0], sems.at[1], root)

    @pl.when(z == 0)
    def _():
        all_of(ends_in, ends_sems).wait_recv()
        hop = [jnp.exp(-rate[n] * float(block)) for n in range(modes)]
        leap = [jnp.exp(-rate[n] * row_size) for n in range(modes)]
        total = [ends_out[n] for n in range(modes)]
        keep = ends_out[modes]
        for peer in range(1, ROW):
            k = ends_in[peer - 1, modes]
            keep = keep * k
            total = [total[n] * (hop[n] * k) + ends_in[peer - 1, n] for n in range(modes)]
        for n in range(modes):
            row_out[n] = total[n]
        row_out[modes] = keep

        for back in range(REACH, 0, -1):
            @pl.when(y + back < n_rows)
            def _():
                row_copy(back).start()

        carry_in[...] = jnp.zeros(carry_in.shape, F32)
        for back in range(REACH, 0, -1):
            @pl.when(y >= back)
            def _():
                row_copy(back).wait_recv()
                for n in range(modes):
                    carry_in[n] = (
                        leap[n] * row_in[back - 1, modes] * carry_in[n] + row_in[back - 1, n]
                    )

        now = [carry_in[n] for n in range(modes)]
        for peer in range(1, ROW):
            src = ends_out if peer == 1 else ends_in.at[peer - 2]
            k = src[modes]
            now = [now[n] * (hop[n] * k) + src[n] for n in range(modes)]
            for n in range(modes):
                carry_out[peer - 1, n] = now[n]
            carry_copy(peer).start()

    @pl.when(z > 0)
    def _():
        carry_copy(1).wait_recv()

    before_ids = get(tail_in, 2)
    q_first = first_two(0, get(tail_q_in, 0), token(0, 0), token(0, 1), before_ids, id_0, id_1)
    state = [carry_in[n] * flag(before_ids[1] == id_0) for n in range(modes)]
    for t in (0, 1):
        if t == 1:
            joined = flag(id_0 == id_1)
            state = [state[n] * joined for n in range(modes)]
        state = [jnp.exp(-rate[n]) * state[n] + gated[t] for n in range(modes)]
        long = tree_sum([resid[n] * state[n] for n in range(modes)])
        base[t] = q_first[t] * (long + skip_in[...] * gated[t])
        live_q[t] = zero

    def out_step(c, part):
        decay = [jnp.exp(-rate[n]) for n in range(modes)]
        for d in range(CHUNK):
            t = c * CHUNK + d
            part = [decay[n] * part[n] for n in range(modes)]
            out_x[pl.ds(t, GROUPS, stride=pitch), :] = base[t] + live_q[t] * tree_sum(list(part))
        for j in range(GROUPS):
            rows = pl.ds(pl.multiple_of(c * CHUNK, CHUNK), CHUNK)
            piece = out_x[pl.ds(j * pitch + pl.multiple_of(c * CHUNK, CHUNK), CHUNK), :]
            out[rows, j * LANES : (j + 1) * LANES] = piece.astype(BF16)
        return part

    lax.fori_loop(
        0, block // CHUNK, out_step, [resid[n] * jnp.exp(2.0 * rate[n]) * state[n] for n in range(modes)]
    )

    @pl.when(me < n_ctx - 1)
    def _():
        tail.wait_send()
        tail_q.wait_send()

    @pl.when(z == SPLIT - 1)
    def _():
        forward.wait_send()

    @pl.when(z == SPLIT)
    def _():
        head.wait_send()
        lift.wait_send()

    @pl.when(prompt)
    def _():
        ends.wait_send()

    @pl.when(z == 0)
    def _():
        for back in range(1, REACH + 1):
            @pl.when(y + back < n_rows)
            def _():
                row_copy(back).wait_send()

        all_of(carry_out, carry_sems).wait_send()


def on_device(n_ctx, query, keyed, valued, short_taps, rates, residues, skip_gain, doc_ids):
    block, channels = query.shape
    modes = rates.shape[0]
    assert channels == GROUPS * LANES and block % CHUNK == 0 and modes == 8
    pitch = block + 8
    tile, twice = (GROUPS, LANES), (2 * GROUPS, LANES)
    dma = pltpu.SemaphoreType.DMA
    hbm = pl.BlockSpec(memory_space=pltpu.HBM)
    return pl.pallas_call(
        functools.partial(kernel, n_ctx, pitch),
        out_shape=pltpu.VMEM(query.shape, BF16),
        in_specs=[hbm] * 8,
        out_specs=pl.BlockSpec(memory_space=pltpu.VMEM),
        scratch_shapes=[
            pltpu.VMEM((3, block, channels), BF16),
            pltpu.VMEM((3, GROUPS * pitch, LANES), F32),
            pltpu.VMEM(short_taps.shape, F32),
            pltpu.VMEM(rates.shape, F32),
            pltpu.VMEM(residues.shape, F32),
            pltpu.VMEM(tile, F32),
            pltpu.SMEM((block,), jnp.int32),
            pltpu.VMEM((GROUPS * 32, LANES), F32),
            pltpu.VMEM((9, *tile), F32),
            pltpu.VMEM((modes, *tile), F32),
            pltpu.VMEM((modes, *tile), F32),
            pltpu.VMEM((block, *tile), F32),
            pltpu.VMEM((block, *tile), F32),
            pltpu.VMEM((block, *tile), F32),
            pltpu.VMEM((GROUPS * pitch, LANES), F32),
            pltpu.VMEM((3, *twice), BF16),
            pltpu.VMEM((3, *twice), BF16),
            pltpu.VMEM((1, *twice), BF16),
            pltpu.VMEM((1, *twice), BF16),
            pltpu.VMEM((4, *twice), BF16),
            pltpu.VMEM((4, *twice), BF16),
            pltpu.VMEM((modes + 1, *tile), F32),
            pltpu.VMEM((ROW - 1, modes + 1, *tile), F32),
            pltpu.VMEM((modes + 1, *tile), F32),
            pltpu.VMEM((modes + 1, *tile), F32),
            pltpu.VMEM((REACH, modes + 1, *tile), F32),
            pltpu.VMEM((ROW - 1, modes, *tile), F32),
            pltpu.VMEM((modes, *tile), F32),
            dma((8,)),
            dma((2,)),
            dma((2,)),
            dma((2,)),
            dma((2,)),
            dma,
            dma((2,)),
            dma((REACH,)),
            dma((REACH,)),
            dma((2,)),
        ],
        compiler_params=pltpu.CompilerParams(
            collective_id=0, has_side_effects=True, vmem_limit_bytes=60 * 1024 * 1024
        ),
    )(
        query, keyed, valued, short_taps, rates, residues,
        skip_gain.reshape(tile), doc_ids,
    )


def solution(mesh):
    return jax.shard_map(
        functools.partial(on_device, mesh.shape["ctx"]),
        mesh=mesh,
        in_specs=(
            P("ctx", "tp"),
            P("ctx", "tp"),
            P("ctx", "tp"),
            P(None, None, "tp"),
            P(None, "tp"),
            P(None, "tp"),
            P("tp"),
            P("ctx"),
        ),
        out_specs=P("ctx", "tp"),
        check_vma=False,
    )
```

time: 34.3 us -> 26.5 us (0.77)
  local copies, waits for them, and re-layouts: 7.21 us -> 0.71 us
  Pallas kernels: 26.6 us -> 25.6 us
    unnamed x17 -> x1, local copies, waits for them, and re-layouts: 7.21 us -> 0.71 us
    pallas_call x1, Pallas kernels: 26.6 us -> 25.6 us  [on_device(): pl.pallas_call(functools.partial(kernel, n_ctx, pitch), out_shape=pltpu.V...]
where the time goes in v2:
time: 26.5 us; the launch traced here: 26.4 us
  Pallas kernels  25.6 us (97%)
  local copies, waits for them, and re-layouts  0.71 us (3%)
    pallas_call x1, Pallas kernels, on_device(): pl.pallas_call(functools.partial(kernel, n_ctx, pitch), out_shape=pltpu.V...  25.6 us
    unnamed x1, local copies, waits for them, and re-layouts  0.71 us

profile of v2, /device:TPU:54, one launch (start us, length us, event | category | flops | bytes accessed | tf_op | source)
XLA Modules:
  0.0 26.4 jit_solution(12238631618722612968)
XLA Ops:
  0.0 25.6 %shard_map.82 = bf16[128,1024]{1,0:T(8,128)(2,1)S(1)} custom-call(bf16[128,1024]{1,0:T(8,128)(2,1)} %q_hbm.1, bf16[128,1024]{1,0:T(8,128)(2,1)} %k_hbm.1, bf16[128,1024]{1,0:T(8,128)(2,1)} %v_hbm.1, f32[3,3,1024]{2,1,0:T(4,128)} %taps_hbm.1, f32[8,1024]{1,0:T(8,128)} %rates_hbm.1, f32[8,1024]{1,0:T(8,128)} %resid_hbm.1, f32[8,128]{1,0:T(8,128)} %bitcast.1, ...), custom_call_target="tpu_custom_call" | custom-call | tf_op jit(solution)/shard_map/pallas_call | solution.py:430
  25.7 0.7 %copy.10 = bf16[128,1024]{1,0:T(8,128)(2,1)} copy(bf16[128,1024]{1,0:T(8,128)(2,1)S(1)} %shard_map.82) | data formatting | bytes 524288

commit v3 on v2

--- a/solution.py
+++ b/solution.py
@@ -15,7 +15,7 @@
 LANES = 128
 GROUPS = 8
 STEP = 8
-CHUNK = 16
+CHUNK = 64
 SPLIT = 4
 
 
@@ -34,7 +34,7 @@
     q_hbm, k_hbm, v_hbm, taps_hbm, rates_hbm, resid_hbm, skip_hbm, ids_hbm,
     out,
     raw, xs, taps_in, rates_in, resid_in, skip_in, ids,
-    prm, taps, rate, resid,
+    prm, taps, rate, resid, power,
     gated, base, live_q, out_x,
     tail_out, tail_in, tail_q_out, tail_q_in, head_out, head_in,
     ends_out, ends_in, relay, row_out, row_in, carry_out, carry_in,
@@ -154,12 +154,13 @@
                 prm[pl.ds(j * 32 + 16 + 3 * s + tap, 1), :] = taps_in[s, pl.ds(tap, 1), cols]
     for n in range(modes):
         rate[n] = prm[pl.ds(n, GROUPS, stride=32), :]
+        power[0, n] = jnp.exp(-rate[n])
     for i in range(9):
         taps[i] = prm[pl.ds(16 + i, GROUPS, stride=32), :]
 
     def ends_step(i, carry):
         k1, k2, v1, v2, *state = carry
-        decay = [jnp.exp(-rate[n]) for n in range(modes)]
+        decay = [power[0, n] for n in range(modes)]
         t0 = i * STEP
         for d in range(STEP):
             t = t0 + d
@@ -182,6 +183,9 @@
     for n in range(modes):
         ends_out[n] = state[n]
     ends_out[modes] = zero
+    for i, steps in ((1, block - 2), (2, block), (3, ROW * block)):
+        for n in range(modes):
+            power[i, n] = jnp.exp(-rate[n] * float(steps))
 
     @pl.when(late)
     def _():
@@ -217,8 +221,8 @@
     def add_first(ref, g, id_near, id0, id1, end_id):
         joined, ending = flag(id0 == id1), flag(id1 == end_id)
         for n in range(modes):
-            first = jnp.exp(-rate[n]) * (g[0] * joined) + g[1]
-            ref[n] += jnp.exp(-rate[n] * float(block - 2)) * (first * ending)
+            first = power[0, n] * (g[0] * joined) + g[1]
+            ref[n] += power[1, n] * (first * ending)
         ref[modes] = flag(id_near == id0) * flag(id0 == end_id)
 
     def own_first():
@@ -252,7 +256,7 @@
 
     def local_step(i, carry):
         q1, q2, *state = carry
-        decay = [jnp.exp(-rate[n]) for n in range(modes)]
+        decay = [power[0, n] for n in range(modes)]
         weight = [resid[n] for n in range(modes)]
         t0 = i * STEP
         for d in range(STEP):
@@ -304,8 +308,6 @@
     def _():
         tail_q.wait_recv()
 
-    row_size = float(ROW * block)
-
     def row_copy(back):
         return remote(
             row_out, row_in.at[back - 1], row_send.at[back - 1], row_recv.at[back - 1],
@@ -323,8 +325,8 @@
     @pl.when(z == 0)
     def _():
         all_of(ends_in, ends_sems).wait_recv()
-        hop = [jnp.exp(-rate[n] * float(block)) for n in range(modes)]
-        leap = [jnp.exp(-rate[n] * row_size) for n in range(modes)]
+        hop = [power[2, n] for n in range(modes)]
+        leap = [power[3, n] for n in range(modes)]
         total = [ends_out[n] for n in range(modes)]
         keep = ends_out[modes]
         for peer in range(1, ROW):
@@ -335,10 +337,13 @@
             row_out[n] = total[n]
         row_out[modes] = keep
 
-        for back in range(REACH, 0, -1):
-            @pl.when(y + back < n_rows)
+        orders = {0: (1, 2, 3, 4), 1: (1, 2, 4, 3), 2: (4, 1, 3, 2), 3: (4, 3, 2, 1)}
+        for at_row in range(n_rows):
+            @pl.when(y == at_row)
             def _():
-                row_copy(back).start()
+                for back in orders.get(at_row, (3, 2, 1)):
+                    if at_row + back < n_rows:
+                        row_copy(back).start()
 
         carry_in[...] = jnp.zeros(carry_in.shape, F32)
         for back in range(REACH, 0, -1):
@@ -370,13 +375,13 @@
         if t == 1:
             joined = flag(id_0 == id_1)
             state = [state[n] * joined for n in range(modes)]
-        state = [jnp.exp(-rate[n]) * state[n] + gated[t] for n in range(modes)]
+        state = [power[0, n] * state[n] + gated[t] for n in range(modes)]
         long = tree_sum([resid[n] * state[n] for n in range(modes)])
         base[t] = q_first[t] * (long + skip_in[...] * gated[t])
         live_q[t] = zero
 
     def out_step(c, part):
-        decay = [jnp.exp(-rate[n]) for n in range(modes)]
+        decay = [power[0, n] for n in range(modes)]
         for d in range(CHUNK):
             t = c * CHUNK + d
             part = [decay[n] * part[n] for n in range(modes)]
@@ -444,6 +449,7 @@
             pltpu.VMEM((9, *tile), F32),
             pltpu.VMEM((modes, *tile), F32),
             pltpu.VMEM((modes, *tile), F32),
+            pltpu.VMEM((4, modes, *tile), F32),
             pltpu.VMEM((block, *tile), F32),
             pltpu.VMEM((block, *tile), F32),
             pltpu.VMEM((block, *tile), F32),

time: 26.5 us -> 26.5 us (level)
  the two profiles are of different devices: /device:TPU:54 before, /device:TPU:46 now
where the time goes in v3:
time: 26.5 us; the launch traced here: 26.4 us
  Pallas kernels  25.7 us (97%)
  local copies, waits for them, and re-layouts  0.71 us (3%)
    pallas_call x1, Pallas kernels, on_device(): pl.pallas_call(functools.partial(kernel, n_ctx, pitch), out_shape=pltpu.V...  25.7 us
    unnamed x1, local copies, waits for them, and re-layouts  0.71 us

profile of v3, /device:TPU:46, one launch (start us, length us, event | category | flops | bytes accessed | tf_op | source)
XLA Modules:
  0.0 26.4 jit_solution(11622361020775946841)
XLA Ops:
  0.0 25.7 %shard_map.82 = bf16[128,1024]{1,0:T(8,128)(2,1)S(1)} custom-call(bf16[128,1024]{1,0:T(8,128)(2,1)} %q_hbm.1, bf16[128,1024]{1,0:T(8,128)(2,1)} %k_hbm.1, bf16[128,1024]{1,0:T(8,128)(2,1)} %v_hbm.1, f32[3,3,1024]{2,1,0:T(4,128)} %taps_hbm.1, f32[8,1024]{1,0:T(8,128)} %rates_hbm.1, f32[8,1024]{1,0:T(8,128)} %resid_hbm.1, f32[8,128]{1,0:T(8,128)} %bitcast.1, ...), custom_call_target="tpu_custom_call" | custom-call | tf_op jit(solution)/shard_map/pallas_call | solution.py:435
  25.7 0.7 %copy.10 = bf16[128,1024]{1,0:T(8,128)(2,1)} copy(bf16[128,1024]{1,0:T(8,128)(2,1)S(1)} %shard_map.82) | data formatting | bytes 524288

commit v4 on v3

--- a/solution.py
+++ b/solution.py
@@ -37,8 +37,8 @@
     prm, taps, rate, resid, power,
     gated, base, live_q, out_x,
     tail_out, tail_in, tail_q_out, tail_q_in, head_out, head_in,
-    ends_out, ends_in, relay, row_out, row_in, carry_out, carry_in,
-    load_sem, tail_sems, tail_q_sems, head_sems, lift_sems, forward_send, ends_sems,
+    ends_out, ends_in, relay, relay_in, row_out, row_in, carry_out, carry_in,
+    load_sem, tail_sems, tail_q_sems, head_sems, forward_sems, ends_sems,
     row_send, row_recv, carry_sems,
 ):
     block = q_hbm.shape[0]
@@ -67,8 +67,7 @@
     @pl.when(z == 0)
     def _():
         for peer in range(1, ROW):
-            if peer != SPLIT:
-                greet(root + peer)
+            greet(root + peer)
         for back in range(1, REACH + 1):
             @pl.when(y >= back)
             def _():
@@ -132,7 +131,7 @@
     def enter():
         rows_ahead = jnp.minimum(REACH, n_rows - 1 - y)
         expected = jnp.where(me < n_ctx - 1, 1, 0) + jnp.where(z == 0, rows_ahead, 1)
-        pl.semaphore_wait(barrier, expected)
+        pl.semaphore_wait(barrier, expected + jnp.where(z == SPLIT, 1, 0))
 
         @pl.when(me < n_ctx - 1)
         def _():
@@ -193,15 +192,14 @@
 
     lifter = root + SPLIT - 1
     head = remote(head_out, head_in, head_sems.at[0], head_sems.at[1], lifter)
-    lift = remote(ends_out, relay, lift_sems.at[0], lift_sems.at[1], lifter)
-    forward = remote(relay, ends_in.at[SPLIT - 1], forward_send, ends_sems.at[1], root)
+    forward = remote(relay, relay_in, forward_sems.at[0], forward_sems.at[1], root)
     slot = lax.rem(z + ROW - 1, ROW)
     ends = remote(ends_out, ends_in.at[slot], ends_sems.at[0], ends_sems.at[1], root)
 
     @pl.when(z == SPLIT)
     def _():
         head.start()
-        lift.start()
+        ends.start()
 
     def first_two(s, before, x0, x1, before_ids, id0, id1):
         far, near = before
@@ -298,7 +296,7 @@
     @pl.when(z == SPLIT - 1)
     def _():
         head.wait_recv()
-        lift.wait_recv()
+        relay[...] = jnp.zeros(relay.shape, F32)
         (head_0, head_1), (head_end, _) = get(head_in, 2), get(head_in, 3)
         first = first_gated(tail_out, get(head_in, 0), get(head_in, 1), head_0, head_1)
         add_first(relay, first, id_end, head_0, head_1, head_end)
@@ -324,7 +322,10 @@
 
     @pl.when(z == 0)
     def _():
+        forward.wait_recv()
         all_of(ends_in, ends_sems).wait_recv()
+        for n in range(modes + 1):
+            ends_in[SPLIT - 1, n] += relay_in[n]
         hop = [power[2, n] for n in range(modes)]
         leap = [power[3, n] for n in range(modes)]
         total = [ends_out[n] for n in range(modes)]
@@ -408,9 +409,8 @@
     @pl.when(z == SPLIT)
     def _():
         head.wait_send()
-        lift.wait_send()
-
-    @pl.when(prompt)
+
+    @pl.when(z > 0)
     def _():
         ends.wait_send()
 
@@ -464,6 +464,7 @@
             pltpu.VMEM((ROW - 1, modes + 1, *tile), F32),
             pltpu.VMEM((modes + 1, *tile), F32),
             pltpu.VMEM((modes + 1, *tile), F32),
+            pltpu.VMEM((modes + 1, *tile), F32),
             pltpu.VMEM((REACH, modes + 1, *tile), F32),
             pltpu.VMEM((ROW - 1, modes, *tile), F32),
             pltpu.VMEM((modes, *tile), F32),
@@ -472,7 +473,6 @@
             dma((2,)),
             dma((2,)),
             dma((2,)),
-            dma,
             dma((2,)),
             dma((REACH,)),
             dma((REACH,)),

time: 26.5 us -> 26.4 us (level)
  no operation moved by 1% of the time
where the time goes in v4:
time: 26.4 us; the launch traced here: 26.3 us
  Pallas kernels  25.6 us (97%)
  local copies, waits for them, and re-layouts  0.71 us (3%)
    pallas_call x1, Pallas kernels, on_device(): pl.pallas_call(functools.partial(kernel, n_ctx, pitch), out_shape=pltpu.V...  25.6 us
    unnamed x1, local copies, waits for them, and re-layouts  0.71 us

profile of v4, /device:TPU:46, one launch (start us, length us, event | category | flops | bytes accessed | tf_op | source)
XLA Modules:
  0.0 26.3 jit_solution(5265423674994480051)
XLA Ops:
  0.0 25.6 %shard_map.82 = bf16[128,1024]{1,0:T(8,128)(2,1)S(1)} custom-call(bf16[128,1024]{1,0:T(8,128)(2,1)} %q_hbm.1, bf16[128,1024]{1,0:T(8,128)(2,1)} %k_hbm.1, bf16[128,1024]{1,0:T(8,128)(2,1)} %v_hbm.1, f32[3,3,1024]{2,1,0:T(4,128)} %taps_hbm.1, f32[8,1024]{1,0:T(8,128)} %rates_hbm.1, f32[8,1024]{1,0:T(8,128)} %resid_hbm.1, f32[8,128]{1,0:T(8,128)} %bitcast.1, ...), custom_call_target="tpu_custom_call" | custom-call | tf_op jit(solution)/shard_map/pallas_call | solution.py:435
  25.6 0.7 %copy.10 = bf16[128,1024]{1,0:T(8,128)(2,1)} copy(bf16[128,1024]{1,0:T(8,128)(2,1)S(1)} %shard_map.82) | data formatting | bytes 524288

commit v5 on v4

--- a/solution.py
+++ b/solution.py
@@ -308,7 +308,9 @@
 
     def row_copy(back):
         return remote(
-            row_out, row_in.at[back - 1], row_send.at[back - 1], row_recv.at[back - 1],
+            row_out.at[pl.ds(0, modes + (back < REACH))],
+            row_in.at[back - 1, pl.ds(0, modes + (back < REACH))],
+            row_send.at[back - 1], row_recv.at[back - 1],
             lax.rem(me + back * ROW, n_ctx),
         )
 
@@ -352,9 +354,12 @@
             def _():
                 row_copy(back).wait_recv()
                 for n in range(modes):
-                    carry_in[n] = (
-                        leap[n] * row_in[back - 1, modes] * carry_in[n] + row_in[back - 1, n]
-                    )
+                    if back == REACH:
+                        carry_in[n] = row_in[back - 1, n]
+                    else:
+                        carry_in[n] = (
+                            leap[n] * row_in[back - 1, modes] * carry_in[n] + row_in[back - 1, n]
+                        )
 
         now = [carry_in[n] for n in range(modes)]
         for peer in range(1, ROW):

time: 26.4 us -> 26.3 us (level)
  the two profiles are of different devices: /device:TPU:46 before, /device:TPU:62 now
where the time goes in v5:
time: 26.3 us; the launch traced here: 26.2 us
  Pallas kernels  25.5 us (97%)
  local copies, waits for them, and re-layouts  0.71 us (3%)
    pallas_call x1, Pallas kernels, on_device(): pl.pallas_call(functools.partial(kernel, n_ctx, pitch), out_shape=pltpu.V...  25.5 us
    unnamed x1, local copies, waits for them, and re-layouts  0.71 us

profile of v5, /device:TPU:62, one launch (start us, length us, event | category | flops | bytes accessed | tf_op | source)
XLA Modules:
  0.0 26.2 jit_solution(17761109469377786045)
XLA Ops:
  0.0 25.5 %shard_map.82 = bf16[128,1024]{1,0:T(8,128)(2,1)S(1)} custom-call(bf16[128,1024]{1,0:T(8,128)(2,1)} %q_hbm.1, bf16[128,1024]{1,0:T(8,128)(2,1)} %k_hbm.1, bf16[128,1024]{1,0:T(8,128)(2,1)} %v_hbm.1, f32[3,3,1024]{2,1,0:T(4,128)} %taps_hbm.1, f32[8,1024]{1,0:T(8,128)} %rates_hbm.1, f32[8,1024]{1,0:T(8,128)} %resid_hbm.1, f32[8,128]{1,0:T(8,128)} %bitcast.1, ...), custom_call_target="tpu_custom_call" | custom-call | tf_op jit(solution)/shard_map/pallas_call | solution.py:440
  25.5 0.7 %copy.10 = bf16[128,1024]{1,0:T(8,128)(2,1)} copy(bf16[128,1024]{1,0:T(8,128)(2,1)S(1)} %shard_map.82) | data formatting | bytes 524288

commit v6 on v5

--- a/solution.py
+++ b/solution.py
@@ -14,8 +14,8 @@
 REACH = 4
 LANES = 128
 GROUPS = 8
-STEP = 8
-CHUNK = 64
+STEP = 16
+CHUNK = 128
 SPLIT = 4
 
 

time: 26.3 us -> 25.9 us (0.985)
  the two profiles are of different devices: /device:TPU:62 before, /device:TPU:46 now
where the time goes in v6:
time: 25.9 us; the launch traced here: 25.7 us
  Pallas kernels  25 us (97%)
  local copies, waits for them, and re-layouts  0.71 us (3%)
    pallas_call x1, Pallas kernels, on_device(): pl.pallas_call(functools.partial(kernel, n_ctx, pitch), out_shape=pltpu.V...  25 us
    unnamed x1, local copies, waits for them, and re-layouts  0.71 us

profile of v6, /device:TPU:46, one launch (start us, length us, event | category | flops | bytes accessed | tf_op | source)
XLA Modules:
  0.0 25.7 jit_solution(14625492402097296060)
XLA Ops:
  0.0 25.0 %shard_map.82 = bf16[128,1024]{1,0:T(8,128)(2,1)S(1)} custom-call(bf16[128,1024]{1,0:T(8,128)(2,1)} %q_hbm.1, bf16[128,1024]{1,0:T(8,128)(2,1)} %k_hbm.1, bf16[128,1024]{1,0:T(8,128)(2,1)} %v_hbm.1, f32[3,3,1024]{2,1,0:T(4,128)} %taps_hbm.1, f32[8,1024]{1,0:T(8,128)} %rates_hbm.1, f32[8,1024]{1,0:T(8,128)} %resid_hbm.1, f32[8,128]{1,0:T(8,128)} %bitcast.1, ...), custom_call_target="tpu_custom_call" | custom-call | tf_op jit(solution)/shard_map/pallas_call | solution.py:440
  25.0 0.7 %copy.10 = bf16[128,1024]{1,0:T(8,128)(2,1)} copy(bf16[128,1024]{1,0:T(8,128)(2,1)S(1)} %shard_map.82) | data formatting | bytes 524288

commit v7 on v6

--- a/solution.py
+++ b/solution.py
@@ -14,7 +14,7 @@
 REACH = 4
 LANES = 128
 GROUPS = 8
-STEP = 16
+STEP = 32
 CHUNK = 128
 SPLIT = 4
 

time: 25.9 us -> 25.8 us (level)
  no operation moved by 1% of the time
where the time goes in v7:
time: 25.8 us; the launch traced here: 25.7 us
  Pallas kernels  25 us (97%)
  local copies, waits for them, and re-layouts  0.71 us (3%)
    pallas_call x1, Pallas kernels, on_device(): pl.pallas_call(functools.partial(kernel, n_ctx, pitch), out_shape=pltpu.V...  25 us
    unnamed x1, local copies, waits for them, and re-layouts  0.71 us

profile of v7, /device:TPU:46, one launch (start us, length us, event | category | flops | bytes accessed | tf_op | source)
XLA Modules:
  0.0 25.7 jit_solution(3680873913628251428)
XLA Ops:
  0.0 25.0 %shard_map.82 = bf16[128,1024]{1,0:T(8,128)(2,1)S(1)} custom-call(bf16[128,1024]{1,0:T(8,128)(2,1)} %q_hbm.1, bf16[128,1024]{1,0:T(8,128)(2,1)} %k_hbm.1, bf16[128,1024]{1,0:T(8,128)(2,1)} %v_hbm.1, f32[3,3,1024]{2,1,0:T(4,128)} %taps_hbm.1, f32[8,1024]{1,0:T(8,128)} %rates_hbm.1, f32[8,1024]{1,0:T(8,128)} %resid_hbm.1, f32[8,128]{1,0:T(8,128)} %bitcast.1, ...), custom_call_target="tpu_custom_call" | custom-call | tf_op jit(solution)/shard_map/pallas_call | solution.py:440
  25.0 0.7 %copy.10 = bf16[128,1024]{1,0:T(8,128)(2,1)} copy(bf16[128,1024]{1,0:T(8,128)(2,1)S(1)} %shard_map.82) | data formatting | bytes 524288
